TPU v7x, 512 devices: a whole 4x8x8 slice. The times are simulated.
512 devices in a mesh: section: 16 (over x_lo, z), dp: 32 (over x_hi, y, core).
Axes of the slice: x: 4 (x_hi: 2, x_lo: 2; x = x_hi * 2 + x_lo), y: 8, z: 8, core: 2. Of those that a mesh axis runs over, the one named last changes fastest.
Arguments:
- acts_down: bfloat16 [3, 16, 32, 16, 16, 256], P(None, 'section', 'dp'), may hold values from -6 to 6
- acts_up: bfloat16 [3, 16, 32, 16, 16, 256], P(None, 'section', 'dp'), may hold values from -6 to 6
- front_down: bfloat16 [16, 32, 16, 16, 256], P('section', 'dp'), may hold values from -6 to 6
- front_up: bfloat16 [16, 32, 16, 16, 256], P('section', 'dp'), may hold values from -6 to 6
- master: float32 [16, 2304, 256], P('section', 'dp'), may hold values from -4 to 4
- moment_first: float32 [16, 2304, 256], P('section', 'dp'), may hold values from -36 to 36
- moment_second: float32 [16, 2304, 256], P('section', 'dp'), may hold values from 10 to 100
Outputs:
- dx_down: bfloat16 [3, 16, 32, 16, 16, 256], P(None, 'section', 'dp')
- dx_up: bfloat16 [3, 16, 32, 16, 16, 256], P(None, 'section', 'dp')
- new_weight: bfloat16 [16, 2304, 256], P('section', 'dp')
- new_master: float32 [16, 2304, 256], P('section', 'dp')
- new_first: float32 [16, 2304, 256], P('section', 'dp')
- new_second: float32 [16, 2304, 256], P('section', 'dp')
All inputs are finite; a program needn't handle non-finite values.
Results may differ from a plain program's by a relative error of at most 0.0025.
The roundings to bfloat16 on the way count: a program that leaves them out, or rounds other values in their place, can miss the bound.
Values may be sent and summed in bfloat16 or wider, within the bound.
No kernel may reach another device: no remote copies, remote signals or barrier semaphores. Data moves between devices by JAX's collectives and lax.ppermute only.
A program may use at most 64 MiB of HBM per device.

v0:
```python
import jax
import jax.numpy as jnp
from jax import lax
from jax.sharding import PartitionSpec as P

TICKS = 3
beta_first = 0.9
beta_second = 0.95
learn_rate = 0.01
decay_rate = 0.1
epsilon = 1e-08


def from_partner(value, axis, stride):
    return lax.ppermute(value, axis, [(i, i ^ 1 << stride) for i in range(lax.axis_size(axis))])


def passed_along(value, axis, by):
    length = lax.axis_size(axis)
    pairs = [(i, i + by) for i in range(length) if 0 <= i + by < length]
    return lax.ppermute(value, axis, pairs)


def shifted_taps(feature, direction):
    images, height, columns, channels = feature.shape
    padded = jnp.pad(feature, ((0, 0), (1, 1), (1, 1), (0, 0)))
    pieces = []
    for row_step in range(3):
        for col_step in range(3):
            row_start = 1 + direction * (row_step - 1)
            col_start = 1 + direction * (col_step - 1)
            pieces.append(
                padded[:, row_start : row_start + height, col_start : col_start + columns, :]
            )
    return jnp.concatenate(pieces, axis=3).reshape(images * height * columns, 9 * channels)


def section_front(inputs, incoming, weight):
    channels = inputs.shape[-1]
    factor = (9 * channels) ** (-0.5)
    taps_front = shifted_taps(incoming, -1).reshape(-1, 9, channels)
    kernel = weight.reshape(9, channels, channels)
    grad_hidden = lax.dot_general(
        taps_front, kernel, (((1, 2), (0, 2)), ((), ())), preferred_element_type=jnp.float32
    )
    grad_hidden = factor * grad_hidden.reshape(inputs.shape)
    widened = inputs.astype(jnp.float32)
    hidden, pullback = jax.vjp(jax.nn.gelu, widened)
    outgoing = (incoming.astype(jnp.float32) + pullback(grad_hidden)[0]).astype(jnp.bfloat16)
    return (outgoing, hidden.astype(jnp.bfloat16))


def weight_term(hiddens, seen):
    channels = hiddens[0].shape[-1]
    factor = (9 * channels) ** (-0.5)
    summed = jnp.zeros((9 * channels, channels), jnp.float32)
    for hidden, incoming in zip(hiddens, seen):
        taps_hidden = shifted_taps(hidden, 1)
        summed = summed + lax.dot_general(
            taps_hidden,
            incoming.reshape(-1, channels),
            (((0,), (0,)), ((), ())),
            preferred_element_type=jnp.float32,
        )
    return factor * summed


def per_device(acts_down, acts_up, front_down, front_up, master, moment_first, moment_second):
    sections = lax.axis_size("section")
    own_rows = master[0].astype(jnp.bfloat16)
    mirror_rows = own_rows
    for bit_number in range(sections.bit_length() - 1):
        mirror_rows = from_partner(mirror_rows, "section", bit_number)
    own_weight, mirror_weight = (
        lax.all_gather(own_rows, "dp", axis=0, tiled=True),
        lax.all_gather(mirror_rows, "dp", axis=0, tiled=True),
    )
    grad_down = front_down[0]
    grad_up = front_up[0]
    seen_down = []
    seen_up = []
    hidden_down = []
    hidden_up = []
    outs_down = []
    outs_up = []
    for tick_index in range(TICKS):
        seen_down.append(grad_down)
        seen_up.append(grad_up)
        next_down, hid_down = section_front(acts_down[tick_index, 0], grad_down, own_weight)
        next_up, hid_up = section_front(acts_up[tick_index, 0], grad_up, mirror_weight)
        hidden_down.append(hid_down)
        hidden_up.append(hid_up)
        outs_down.append(next_down)
        outs_up.append(next_up)
        if tick_index + 1 < TICKS:
            grad_down = passed_along(next_down, "section", -1)
            grad_up = passed_along(next_up, "section", 1)
    term_down = weight_term(hidden_down, seen_down)
    term_up = weight_term(hidden_up, seen_up)
    full_down, full_up = (
        lax.psum(term_down.astype(jnp.bfloat16), "dp").astype(jnp.float32),
        lax.psum(term_up.astype(jnp.bfloat16), "dp").astype(jnp.float32),
    )
    shard_rows = term_down.shape[0] // lax.axis_size("dp")
    row_start = lax.axis_index("dp") * shard_rows
    down_rows = lax.dynamic_slice_in_dim(full_down, row_start, shard_rows, 0)
    up_rows = lax.dynamic_slice_in_dim(full_up, row_start, shard_rows, 0)
    mirror_grad = up_rows
    for bit_number in range(sections.bit_length() - 1):
        mirror_grad = from_partner(mirror_grad.astype(jnp.bfloat16), "section", bit_number).astype(
            mirror_grad.dtype
        )
    gradient = down_rows + mirror_grad
    old_master = master[0]
    new_first = beta_first * moment_first[0] + (1.0 - beta_first) * gradient
    new_second = beta_second * moment_second[0] + (1.0 - beta_second) * gradient * gradient
    new_master = old_master - learn_rate * (
        new_first / (jnp.sqrt(new_second) + epsilon) + decay_rate * old_master
    )
    return (
        jnp.stack(outs_down)[:, None],
        jnp.stack(outs_up)[:, None],
        new_master.astype(jnp.bfloat16)[None],
        new_master[None],
        new_first[None],
        new_second[None],
    )


def solution(mesh):
    placed = (
        P(None, "section", "dp", None, None, None),
        P(None, "section", "dp", None, None, None),
        P("section", "dp", None, None, None),
        P("section", "dp", None, None, None),
        P("section", "dp", None),
        P("section", "dp", None),
        P("section", "dp", None),
    )
    return jax.shard_map(
        per_device,
        mesh=mesh,
        in_specs=placed,
        out_specs=(
            P(None, "section", "dp", None, None, None),
            P(None, "section", "dp", None, None, None),
            P("section", "dp", None),
            P("section", "dp", None),
            P("section", "dp", None),
            P("section", "dp", None),
        ),
        check_vma=False,
    )
```

profile of v0, /device:TPU:2, one launch (start us, length us, event | category | flops | bytes accessed | tf_op | source)
XLA Modules:
  0.0 534.1 jit_solution(15789119350843120180)
XLA Ops:
  7.2 1.5 bitcast_convert_fusion
  8.8 4.3 collective-permute-start.2
  13.1 1.0 constant_dynamic-update-slice_fusion.8
  14.1 0.9 constant_dynamic-update-slice_fusion.7
  15.0 0.9 constant_dynamic-update-slice_fusion.6
  16.0 0.9 constant_dynamic-update-slice_fusion.5
  17.1 1.0 copy-done.5
  20.6 1.0 copy-done.15
  21.8 0.8 copy-done.3
  22.9 0.8 constant_dynamic-update-slice_fusion.71
  25.1 0.7 constant_dynamic-update-slice_fusion.68
  26.0 0.9 constant_dynamic-update-slice_fusion.67
  27.7 0.8 pad_slice_fusion.40
  31.4 0.8 constant_dynamic-update-slice_fusion.58
  32.8 6.1 %collective-permute-start.3 = (bf16[72,256]{1,0:T(8,128)(2,1)S(1)}, bf16[72,256]{1,0:T(8,128)(2,1)S(1)}, u32[]{:S(2)}, u32[]{:S(2)}) collective-permute-start(bf16[72,256]{1,0:T(8,128)(2,1)S(1)} %collective-permute-done.2), channel_id=1, source_target_pairs={{0,64},{32,96},{64,0},{96,32},{128,192},{160,224},{192,128},{224,1... | collective-permute-start | bytes 110600 | tf_op jit(solution)/shard_map/ppermute | solution.py:15
  39.5 1.2 collective-permute-done.3
  40.8 9.1 %collective-permute-start.4 = (bf16[72,256]{1,0:T(8,128)(2,1)S(1)}, bf16[72,256]{1,0:T(8,128)(2,1)S(1)}, u32[]{:S(2)}, u32[]{:S(2)}) collective-permute-start(bf16[72,256]{1,0:T(8,128)(2,1)S(1)} %collective-permute-done.3), channel_id=1, source_target_pairs={{0,128},{32,160},{64,192},{96,224},{128,0},{160,32},{192,64},{224,... | collective-permute-start | bytes 110600 | tf_op jit(solution)/shard_map/ppermute | solution.py:15
  50.6 1.3 collective-permute-done.4
  51.9 2.8 collective-permute-start.5
  55.4 3.5 dot_general.48
  60.3 3.3 fusion.219
  63.5 35.4 %all-gather.3.cloned.1.call-done = bf16[2304,256]{1,0:T(8,128)(2,1)} async-done(((bf16[72,256]{1,0:T(8,128)(2,1)}), bf16[2304,256]{1,0:T(8,128)(2,1)}) %all-gather.3.cloned.1.call-update) | async-done | bytes 1179664 | tf_op jit(solution)/shard_map/all_gather | solution.py:75
  98.9 2.9 fusion.119
  101.8 6.8 %collective-permute-start = (bf16[1,16,16,256]{3,2,1,0:T(8,128)(2,1)S(1)}, bf16[1,16,16,256]{3,2,1,0:T(8,128)(2,1)S(1)}, u32[]{:S(2)}, u32[]{:S(2)}) collective-permute-start(bf16[1,16,16,256]{3,2,1,0:T(8,128)(2,1)S(1)} %bitcast.548), channel_id=1, source_target_pairs={{32,0},{64,32},{96,64},{128,96},{160,128},{192,160},{224,192},{256... | collective-permute-start | bytes 393224 | tf_op jit(solution)/shard_map/ppermute | solution.py:21
  109.2 3.6 dot_general.54
  113.5 0.7 constant_dynamic-update-slice_fusion.17
  114.3 0.7 constant_dynamic-update-slice_fusion.16
  115.7 0.7 constant_dynamic-update-slice_fusion.14
  119.9 3.5 dot_general.50
  123.4 3.5 fusion.125
  126.9 4.6 collective-permute-start.1
  131.6 51.5 %all-gather.5.cloned.1.call-done = bf16[2304,256]{1,0:T(8,128)(2,1)} async-done(((bf16[72,256]{1,0:T(8,128)(2,1)}), bf16[2304,256]{1,0:T(8,128)(2,1)}) %all-gather.5.cloned.1.call-update) | async-done | bytes 1179664 | tf_op jit(solution)/shard_map/all_gather | solution.py:76
  183.1 3.0 fusion.139
  186.1 3.7 collective-permute-start.6
  189.8 2.0 convolution_bitcast_fusion.2
  191.8 4.9 collective-permute-done.6
  202.3 0.7 constant_dynamic-update-slice_fusion.36
  203.0 3.5 dot_general.56
  206.5 3.0 fusion.145
  209.6 2.1 collective-permute-start.7
  211.7 3.7 fusion.7
  215.3 3.4 collective-permute-done.7
  219.3 1.7 fusion.6
  221.0 0.7 constant_dynamic-update-slice_fusion.26
  223.1 0.7 constant_dynamic-update-slice_fusion.23
  223.9 0.7 constant_dynamic-update-slice_fusion.22
  227.4 2.4 dot_general.52
  229.8 2.2 fusion.211
  232.0 1.7 maximum_bitcast_fusion
  235.8 0.7 constant_dynamic-update-slice_fusion.50
  237.9 0.7 constant_dynamic-update-slice_fusion.47
  238.7 256.8 %all-reduce.15.cloned.1.call-done = (bf16[2304,256]{1,0:T(8,128)(2,1)}, bf16[2304,256]{1,0:T(8,128)(2,1)}) async-done(((bf16[2304,256]{1,0:T(8,128)(2,1)}, bf16[2304,256]{1,0:T(8,128)(2,1)}), (bf16[2304,256]{1,0:T(8,128)(2,1)}, bf16[2304,256]{1,0:T(8,128)(2,1)})) %all-reduce.15.cloned.1.call-update) | async-done | bytes 2359312 | tf_op jit(solution)/shard_map/psum | solution.py:102
  495.4 0.8 convert_convert_fusion
  496.2 3.5 collective-permute-start.8
  500.4 1.6 collective-permute-done.8
  502.0 4.6 collective-permute-start.9
  507.4 2.4 dot_general.58
  509.9 7.3 %collective-permute-start.10 = (bf16[72,256]{1,0:T(8,128)(2,1)S(1)}, bf16[72,256]{1,0:T(8,128)(2,1)S(1)}, u32[]{:S(2)}, u32[]{:S(2)}) collective-permute-start(bf16[72,256]{1,0:T(8,128)(2,1)S(1)} %collective-permute-done.9), channel_id=1, source_target_pairs={{0,128},{32,160},{64,192},{96,224},{128,0},{160,32},{192,64},{224,... | collective-permute-start | bytes 110600 | tf_op jit(solution)/shard_map/ppermute | solution.py:15
  517.2 2.2 fusion.194
  519.4 0.8 collective-permute-done.10
  520.2 2.2 collective-permute-start.11
  522.4 0.8 maximum_bitcast_fusion.1
  523.2 2.8 collective-permute-done.11
  526.0 1.5 convert_bitcast_fusion.8
  (138 shorter events, 32.9 us)
Async XLA Ops:
  7.2 9.8 %copy-start = (bf16[1,1,16,16,256]{4,3,2,1,0:T(8,128)(2,1)S(1)}, bf16[1,1,16,16,256]{4,3,2,1,0:T(8,128)(2,1)}, u32[]{:S(2)}) copy-start(bf16[1,1,16,16,256]{4,3,2,1,0:T(8,128)(2,1)} %param.9) | copy-start | bytes 393220
  7.2 91.8 %all-gather.3.cloned.1.call-start = ((), (), s32[]{:S(2)}) async-start(), calls=%async_computation | async-start | bytes 1216512 | tf_op jit(solution)/shard_map/all_gather | solution.py:75
  8.8 174.3 %all-gather.5.cloned.1.call-start = ((), (), s32[]{:S(2)}) async-start(), calls=%async_computation.1 | async-start | bytes 1216512 | tf_op jit(solution)/shard_map/all_gather | solution.py:76
  8.8 23.9 %collective-permute-start.2 = (bf16[72,256]{1,0:T(8,128)(2,1)}, bf16[72,256]{1,0:T(8,128)(2,1)S(1)}, u32[]{:S(2)}, u32[]{:S(2)}) collective-permute-start(bf16[72,256]{1,0:T(8,128)(2,1)} %bitcast_convert_fusion), channel_id=1, source_target_pairs={{0,32},{32,0},{64,96},{96,64},{128,160},{160,128},{192,224},{224,1... | collective-permute-start | bytes 110600 | tf_op jit(solution)/shard_map/ppermute | solution.py:15
  13.1 5.0 copy-start.1
  17.1 1.0 copy-start.5
  18.1 1.0 copy-start.4
  19.1 1.0 copy-start.6
  20.6 1.0 copy-start.15
  21.6 1.0 copy-start.3
  22.6 3.3 copy-start.13
  32.7 17.9 %copy-start.17 = (bf16[1,16,16,2304]{3,2,1,0:T(8,128)(2,1)}, bf16[1,16,16,2304]{3,2,1,0:T(8,128)(2,1)S(1)}, u32[]{:S(2)}) copy-start(bf16[1,16,16,2304]{3,2,1,0:T(8,128)(2,1)S(1)} %constant_dynamic-update-slice_fusion.72) | copy-start | bytes 3538948
  32.8 8.0 %collective-permute-start.3 = (bf16[72,256]{1,0:T(8,128)(2,1)S(1)}, bf16[72,256]{1,0:T(8,128)(2,1)S(1)}, u32[]{:S(2)}, u32[]{:S(2)}) collective-permute-start(bf16[72,256]{1,0:T(8,128)(2,1)S(1)} %collective-permute-done.2), channel_id=1, source_target_pairs={{0,64},{32,96},{64,0},{96,32},{128,192},{160,224},{192,128},{224,1... | collective-permute-start | bytes 110600 | tf_op jit(solution)/shard_map/ppermute | solution.py:15
  40.8 11.1 %collective-permute-start.4 = (bf16[72,256]{1,0:T(8,128)(2,1)S(1)}, bf16[72,256]{1,0:T(8,128)(2,1)S(1)}, u32[]{:S(2)}, u32[]{:S(2)}) collective-permute-start(bf16[72,256]{1,0:T(8,128)(2,1)S(1)} %collective-permute-done.3), channel_id=1, source_target_pairs={{0,128},{32,160},{64,192},{96,224},{128,0},{160,32},{192,64},{224,... | collective-permute-start | bytes 110600 | tf_op jit(solution)/shard_map/ppermute | solution.py:15
  51.9 7.0 %collective-permute-start.5 = (bf16[72,256]{1,0:T(8,128)(2,1)S(1)}, bf16[72,256]{1,0:T(8,128)(2,1)S(1)}, u32[]{:S(2)}, u32[]{:S(2)}) collective-permute-start(bf16[72,256]{1,0:T(8,128)(2,1)S(1)} %collective-permute-done.4), channel_id=1, source_target_pairs={{0,256},{32,288},{64,320},{96,352},{128,384},{160,416},{192,448},{... | collective-permute-start | bytes 110600 | tf_op jit(solution)/shard_map/ppermute | solution.py:15
  58.9 0.6 copy-start.12
  59.5 435.9 %all-reduce.15.cloned.1.call-start = ((), (), s32[]{:S(2)}) async-start(), calls=%async_computation.2 | async-start | bytes 4718592 | tf_op jit(solution)/shard_map/psum | solution.py:102
  101.8 11.7 %collective-permute-start = (bf16[1,16,16,256]{3,2,1,0:T(8,128)(2,1)S(1)}, bf16[1,16,16,256]{3,2,1,0:T(8,128)(2,1)S(1)}, u32[]{:S(2)}, u32[]{:S(2)}) collective-permute-start(bf16[1,16,16,256]{3,2,1,0:T(8,128)(2,1)S(1)} %bitcast.548), channel_id=1, source_target_pairs={{32,0},{64,32},{96,64},{128,96},{160,128},{192,160},{224,192},{256... | collective-permute-start | bytes 393224 | tf_op jit(solution)/shard_map/ppermute | solution.py:21
  126.9 62.9 %collective-permute-start.1 = (bf16[1,16,16,256]{3,2,1,0:T(8,128)(2,1)}, bf16[1,16,16,256]{3,2,1,0:T(8,128)(2,1)S(1)}, u32[]{:S(2)}, u32[]{:S(2)}) collective-permute-start(bf16[1,16,16,256]{3,2,1,0:T(8,128)(2,1)} %fusion.125), channel_id=1, source_target_pairs={{32,0},{64,32},{96,64},{128,96},{160,128},{192,160},{224,192},{256... | collective-permute-start | bytes 393224 | tf_op jit(solution)/shard_map/ppermute | solution.py:21
  183.1 6.8 %copy-start.18 = (bf16[1,16,16,2304]{3,2,1,0:T(8,128)(2,1)S(1)}, bf16[1,16,16,2304]{3,2,1,0:T(8,128)(2,1)}, u32[]{:S(2)}) copy-start(bf16[1,16,16,2304]{3,2,1,0:T(8,128)(2,1)} %copy-done.17) | copy-start | bytes 3538948
  186.1 10.6 %collective-permute-start.6 = (bf16[1,16,16,256]{3,2,1,0:T(8,128)(2,1)S(1)}, bf16[1,16,16,256]{3,2,1,0:T(8,128)(2,1)S(1)}, u32[]{:S(2)}, u32[]{:S(2)}) collective-permute-start(bf16[1,16,16,256]{3,2,1,0:T(8,128)(2,1)S(1)} %bitcast.546), channel_id=1, source_target_pairs={{0,32},{32,64},{64,96},{96,128},{128,160},{160,192},{192,224},{224... | collective-permute-start | bytes 393224 | tf_op jit(solution)/shard_map/ppermute | solution.py:21
  206.5 5.1 copy-start.2
  209.6 5.8 %copy-start.8 = (bf16[1,16,16,256]{3,2,1,0:T(8,128)(2,1)}, bf16[1,16,16,256]{3,2,1,0:T(8,128)(2,1)S(1)}, u32[]{:S(2)}) copy-start(bf16[1,16,16,256]{3,2,1,0:T(8,128)(2,1)S(1)} %fusion.145) | copy-start | bytes 393220
  209.6 9.2 %copy-start.16 = (bf16[1,16,16,2304]{3,2,1,0:T(8,128)(2,1)S(1)}, bf16[1,16,16,2304]{3,2,1,0:T(8,128)(2,1)}, u32[]{:S(2)}) copy-start(bf16[1,16,16,2304]{3,2,1,0:T(8,128)(2,1)} %copy-done.15) | copy-start | bytes 3538948
  209.6 9.2 %collective-permute-start.7 = (bf16[1,16,16,256]{3,2,1,0:T(8,128)(2,1)S(1)}, bf16[1,16,16,256]{3,2,1,0:T(8,128)(2,1)S(1)}, u32[]{:S(2)}, u32[]{:S(2)}) collective-permute-start(bf16[1,16,16,256]{3,2,1,0:T(8,128)(2,1)S(1)} %fusion.145), channel_id=1, source_target_pairs={{0,32},{32,64},{64,96},{96,128},{128,160},{160,192},{192,224},{224... | collective-permute-start | bytes 393224 | tf_op jit(solution)/shard_map/ppermute | solution.py:21
  215.3 4.0 copy-start.14
  496.2 5.8 %collective-permute-start.8 = (bf16[72,256]{1,0:T(8,128)(2,1)S(1)}, bf16[72,256]{1,0:T(8,128)(2,1)S(1)}, u32[]{:S(2)}, u32[]{:S(2)}) collective-permute-start(bf16[72,256]{1,0:T(8,128)(2,1)S(1)} %convert_convert_fusion), channel_id=1, source_target_pairs={{0,32},{32,0},{64,96},{96,64},{128,160},{160,128},{192,224},{224,1... | collective-permute-start | bytes 110600 | tf_op jit(solution)/shard_map/ppermute | solution.py:15
  502.0 7.8 %collective-permute-start.9 = (bf16[72,256]{1,0:T(8,128)(2,1)S(1)}, bf16[72,256]{1,0:T(8,128)(2,1)S(1)}, u32[]{:S(2)}, u32[]{:S(2)}) collective-permute-start(bf16[72,256]{1,0:T(8,128)(2,1)S(1)} %collective-permute-done.8), channel_id=1, source_target_pairs={{0,64},{32,96},{64,0},{96,32},{128,192},{160,224},{192,128},{224,1... | collective-permute-start | bytes 110600 | tf_op jit(solution)/shard_map/ppermute | solution.py:15
  509.8 12.6 %copy-start.9 = (bf16[1,16,16,256]{3,2,1,0:T(8,128)(2,1)S(1)}, bf16[1,16,16,256]{3,2,1,0:T(8,128)(2,1)}, u32[]{:S(2)}) copy-start(bf16[1,16,16,256]{3,2,1,0:T(8,128)(2,1)} %copy-done.8) | copy-start | bytes 393220
  509.8 16.2 %copy-start.7 = (f32[1,72,256]{2,1,0:T(8,128)S(1)}, f32[1,72,256]{2,1,0:T(8,128)}, u32[]{:S(2)}) copy-start(f32[1,72,256]{2,1,0:T(8,128)} %param.11) | copy-start | bytes 221188
  509.9 16.2 %copy-start.10 = (f32[1,72,256]{2,1,0:T(8,128)S(1)}, f32[1,72,256]{2,1,0:T(8,128)}, u32[]{:S(2)}) copy-start(f32[1,72,256]{2,1,0:T(8,128)} %param.13) | copy-start | bytes 221188
  509.9 16.2 %copy-start.11 = (f32[1,72,256]{2,1,0:T(8,128)S(1)}, f32[1,72,256]{2,1,0:T(8,128)}, u32[]{:S(2)}) copy-start(f32[1,72,256]{2,1,0:T(8,128)} %param.12) | copy-start | bytes 221188
  509.9 10.3 %collective-permute-start.10 = (bf16[72,256]{1,0:T(8,128)(2,1)S(1)}, bf16[72,256]{1,0:T(8,128)(2,1)S(1)}, u32[]{:S(2)}, u32[]{:S(2)}) collective-permute-start(bf16[72,256]{1,0:T(8,128)(2,1)S(1)} %collective-permute-done.9), channel_id=1, source_target_pairs={{0,128},{32,160},{64,192},{96,224},{128,0},{160,32},{192,64},{224,... | collective-permute-start | bytes 110600 | tf_op jit(solution)/shard_map/ppermute | solution.py:15
  520.2 5.8 %collective-permute-start.11 = (bf16[72,256]{1,0:T(8,128)(2,1)S(1)}, bf16[72,256]{1,0:T(8,128)(2,1)S(1)}, u32[]{:S(2)}, u32[]{:S(2)}) collective-permute-start(bf16[72,256]{1,0:T(8,128)(2,1)S(1)} %collective-permute-done.10), channel_id=1, source_target_pairs={{0,256},{32,288},{64,320},{96,352},{128,384},{160,416},{192,448},{... | collective-permute-start | bytes 110600 | tf_op jit(solution)/shard_map/ppermute | solution.py:15
Sparse Core Ops, SparseCore 0:
  11.8 87.0 all-gather.2
  102.8 80.2 all-gather.4
  221.1 274.2 all-reduce.14
where the time goes:
time: 535 us; the launch traced here: 534 us
  waiting for transfers between devices  360 us (67%)
  local copies, waits for them, and re-layouts  65.3 us (12%)
  starting transfers between devices  57.3 us (11%)
  matrix products  28.5 us (5%)
  between operations  14.5 us (3%)
  other arithmetic  8.8 us (2%)
    psum x1, waiting for transfers between devices, per_device(): lax.psum(term_up.astype(jnp.bfloat16), 'dp').astype(jnp.float32)  257 us
    all_gather x1, waiting for transfers between devices, per_device(): lax.all_gather(mirror_rows, 'dp', axis=0, tiled=True)  51.5 us
    unnamed x126, local copies, waits for them, and re-layouts  40.9 us
    ppermute x8, starting transfers between devices, from_partner(): lax.ppermute(value, axis, [(i, i ^ 1 << stride) for i in range(lax.axis_s...  40 us
    all_gather x1, waiting for transfers between devices, per_device(): lax.all_gather(own_rows, 'dp', axis=0, tiled=True)  35.4 us
    dot_general x6, local copies, waits for them, and re-layouts, section_front(): lax.dot_general(taps_front, kernel, (((1, 2), (0, 2)), ((), ())), preferr...  19.1 us
    ppermute x4, starting transfers between devices, passed_along(): return lax.ppermute(value, axis, pairs)  17.2 us
    dot_general x6, matrix products, section_front(): lax.dot_general(taps_front, kernel, (((1, 2), (0, 2)), ((), ())), preferr...  16.9 us
  transfers between devices with their start and end apart: 15, of which 10 were waited for; matrix products, arithmetic and copies ran while one was open for 15% of the time, Pallas kernels for 0%

commit v1 on v0

--- a/solution.py
+++ b/solution.py
@@ -99,7 +99,7 @@
     term_up = weight_term(hidden_up, seen_up)
     full_down, full_up = (
         lax.psum(term_down.astype(jnp.bfloat16), "dp").astype(jnp.float32),
-        lax.psum(term_up.astype(jnp.bfloat16), "dp").astype(jnp.float32),
+        jnp.sum(lax.all_gather(term_up.astype(jnp.bfloat16), "dp"), axis=0).astype(jnp.float32),
     )
     shard_rows = term_down.shape[0] // lax.axis_size("dp")
     row_start = lax.axis_index("dp") * shard_rows

time: 535 us -> 748 us (1.40)
  the two profiles are of different devices: /device:TPU:2 before, /device:TPU:4 now
where the time goes in v1:
time: 748 us; the launch traced here: 747 us
  waiting for transfers between devices  582 us (78%)
  starting transfers between devices  54.1 us (7%)
  local copies, waits for them, and re-layouts  51.8 us (7%)
  matrix products  25.1 us (3%)
  other arithmetic  19.4 us (3%)
  between operations  14.6 us (2%)
    psum x1, waiting for transfers between devices, per_device(): lax.psum(term_down.astype(jnp.bfloat16), 'dp').astype(jnp.float32)  234 us
    all_gather x1, waiting for transfers between devices, per_device(): lax.all_gather(term_up.astype(jnp.bfloat16), 'dp')  206 us
    all_gather x1, waiting for transfers between devices, per_device(): lax.all_gather(mirror_rows, 'dp', axis=0, tiled=True)  73.2 us
    ppermute x8, starting transfers between devices, from_partner(): lax.ppermute(value, axis, [(i, i ^ 1 << stride) for i in range(lax.axis_s...  43.3 us
    all_gather x1, waiting for transfers between devices, per_device(): lax.all_gather(own_rows, 'dp', axis=0, tiled=True)  43.2 us
    unnamed x122, local copies, waits for them, and re-layouts  31.6 us
    dot_general x6, matrix products, section_front(): lax.dot_general(taps_front, kernel, (((1, 2), (0, 2)), ((), ())), preferr...  17 us
  transfers between devices with their start and end apart: 16, of which 14 were waited for; matrix products, arithmetic and copies ran while one was open for 12% of the time, Pallas kernels for 0%

profile of v1, /device:TPU:4, one launch (start us, length us, event | category | flops | bytes accessed | tf_op | source)
XLA Modules:
  0.0 747.2 jit_solution(17761983690800165120)
XLA Ops:
  7.2 0.9 bitcast_convert_fusion
  8.1 4.3 collective-permute-start.2
  12.4 1.9 collective-permute-done.2
  14.3 6.1 collective-permute-start.3
  20.4 1.9 collective-permute-done.3
  22.4 9.3 %collective-permute-start.4 = (bf16[72,256]{1,0:T(8,128)(2,1)S(1)}, bf16[72,256]{1,0:T(8,128)(2,1)S(1)}, u32[]{:S(2)}, u32[]{:S(2)}) collective-permute-start(bf16[72,256]{1,0:T(8,128)(2,1)S(1)} %collective-permute-done.3), channel_id=1, source_target_pairs={{0,128},{32,160},{64,192},{96,224},{128,0},{160,32},{192,64},{224,... | collective-permute-start | bytes 110600 | tf_op jit(solution)/shard_map/ppermute | solution.py:15
  31.6 2.0 collective-permute-done.4
  33.6 3.1 collective-permute-start.5
  36.7 2.7 collective-permute-done.5
  40.9 0.9 constant_dynamic-update-slice_fusion.35
  41.8 0.9 constant_dynamic-update-slice_fusion.34
  42.7 0.9 constant_dynamic-update-slice_fusion.33
  43.7 0.9 constant_dynamic-update-slice_fusion.32
  44.8 1.7 dot_general.54
  47.4 1.0 copy-done.13
  48.8 0.8 copy-done.11
  50.1 73.2 %all-gather.7.cloned.1.call-done = bf16[2304,256]{1,0:T(8,128)(2,1)} async-done(((bf16[72,256]{1,0:T(8,128)(2,1)}), bf16[2304,256]{1,0:T(8,128)(2,1)}) %all-gather.7.cloned.1.call-update) | async-done | bytes 1179664 | tf_op jit(solution)/shard_map/all_gather | solution.py:76
  123.3 2.9 fusion.139
  126.1 3.6 collective-permute-start.6
  131.1 1.7 collective-permute-done.6
  132.8 0.7 constant_dynamic-update-slice_fusion.44
  134.2 0.7 constant_dynamic-update-slice_fusion.42
  139.1 3.6 dot_general.56
  142.6 3.0 fusion.145
  145.7 4.4 collective-permute-start.7
  150.1 2.4 collective-permute-done.7
  153.1 1.7 fusion.6
  154.9 0.8 copy-done.1
  156.0 1.7 dot_general.48
  158.0 0.7 constant_dynamic-update-slice_fusion.71
  159.4 0.7 constant_dynamic-update-slice_fusion.69
  160.9 0.9 constant_dynamic-update-slice_fusion.67
  161.9 0.8 constant_dynamic-update-slice_fusion.66
  162.6 0.8 pad_slice_fusion.40
  164.2 43.2 %all-gather.5.cloned.1.call-done = bf16[2304,256]{1,0:T(8,128)(2,1)} async-done(((bf16[72,256]{1,0:T(8,128)(2,1)}), bf16[2304,256]{1,0:T(8,128)(2,1)}) %all-gather.5.cloned.1.call-update) | async-done | bytes 1179664 | tf_op jit(solution)/shard_map/all_gather | solution.py:75
  207.4 2.9 fusion.119
  210.3 1.5 collective-permute-start
  213.1 4.7 collective-permute-done
  219.2 0.7 constant_dynamic-update-slice_fusion.15
  223.3 0.7 constant_dynamic-update-slice_fusion.9
  224.0 3.7 dot_general.50
  227.7 3.6 fusion.125
  231.2 1.3 collective-permute-start.1
  233.9 4.4 collective-permute-done.1
  239.7 0.7 constant_dynamic-update-slice_fusion.24
  243.8 0.7 constant_dynamic-update-slice_fusion.18
  244.6 3.6 dot_general.52
  248.1 1.8 convolution_bitcast_fusion.2
  249.9 2.9 fusion.7
  252.9 1.3 copy-done.16
  254.2 2.5 fusion.211
  256.7 1.7 maximum_bitcast_fusion
  258.7 205.6 %all-gather.9.cloned.1.call-done = bf16[73728,256]{1,0:T(8,128)(2,1)} async-done(((bf16[2304,256]{1,0:T(8,128)(2,1)}), bf16[73728,256]{1,0:T(8,128)(2,1)}) %all-gather.9.cloned.1.call-update) | async-done | bytes 37748752 | tf_op jit(solution)/shard_map/all_gather | solution.py:102
  464.2 12.7 %reduce_sum.12 = bf16[2304,256]{1,0:T(8,128)(2,1)S(1)} reduce(bf16[32,2304,256]{2,1,0:T(8,128)(2,1)} %bitcast.513, bf16[]{:T(256)} %constant.18.clone.1), dimensions={0}, to_apply=%region_1.2 | reduce | flops 18284544 | bytes 38928384 | tf_op jit(solution)/shard_map/reduce_sum | solution.py:102
  476.9 3.6 collective-permute-start.8
  480.5 2.4 collective-permute-done.8
  482.9 4.6 collective-permute-start.9
  488.3 1.6 collective-permute-done.9
  489.9 8.4 %collective-permute-start.10 = (bf16[72,256]{1,0:T(8,128)(2,1)}, bf16[72,256]{1,0:T(8,128)(2,1)S(1)}, u32[]{:S(2)}, u32[]{:S(2)}) collective-permute-start(bf16[72,256]{1,0:T(8,128)(2,1)} %collective-permute-done.9), channel_id=1, source_target_pairs={{0,128},{32,160},{64,192},{96,224},{128,0},{160,32},{192,64},{224,... | collective-permute-start | bytes 110600 | tf_op jit(solution)/shard_map/ppermute | solution.py:15
  498.3 2.2 fusion.194
  500.6 4.0 collective-permute-start.11
  504.5 0.8 maximum_bitcast_fusion.1
  505.3 233.8 %all-reduce.14.cloned.1.call-done = bf16[2304,256]{1,0:T(8,128)(2,1)} async-done(((bf16[2304,256]{1,0:T(8,128)(2,1)}), bf16[2304,256]{1,0:T(8,128)(2,1)}) %all-reduce.14.cloned.1.call-update) | async-done | bytes 1179664 | tf_op jit(solution)/shard_map/psum | solution.py:101
  739.2 1.5 convert_bitcast_fusion.8
  (138 shorter events, 26.1 us)
Async XLA Ops:
  7.2 37.5 %copy-start = (bf16[1,1,16,16,256]{4,3,2,1,0:T(8,128)(2,1)S(1)}, bf16[1,1,16,16,256]{4,3,2,1,0:T(8,128)(2,1)}, u32[]{:S(2)}) copy-start(bf16[1,1,16,16,256]{4,3,2,1,0:T(8,128)(2,1)} %param.10) | copy-start | bytes 393220
  7.2 116.1 %all-gather.7.cloned.1.call-start = ((), (), s32[]{:S(2)}) async-start(), calls=%async_computation.1 | async-start | bytes 1216512 | tf_op jit(solution)/shard_map/all_gather | solution.py:76
  8.1 32.0 %copy-start.5 = (bf16[72,256]{1,0:T(8,128)(2,1)}, bf16[72,256]{1,0:T(8,128)(2,1)S(1)}, u32[]{:S(2)}) copy-start(bf16[72,256]{1,0:T(8,128)(2,1)S(1)} %bitcast_convert_fusion) | copy-start | bytes 110596
  8.1 6.2 collective-permute-start.2
  14.3 8.0 %collective-permute-start.3 = (bf16[72,256]{1,0:T(8,128)(2,1)S(1)}, bf16[72,256]{1,0:T(8,128)(2,1)S(1)}, u32[]{:S(2)}, u32[]{:S(2)}) collective-permute-start(bf16[72,256]{1,0:T(8,128)(2,1)S(1)} %collective-permute-done.2), channel_id=1, source_target_pairs={{0,64},{32,96},{64,0},{96,32},{128,192},{160,224},{192,128},{224,1... | collective-permute-start | bytes 110600 | tf_op jit(solution)/shard_map/ppermute | solution.py:15
  22.4 11.2 %collective-permute-start.4 = (bf16[72,256]{1,0:T(8,128)(2,1)S(1)}, bf16[72,256]{1,0:T(8,128)(2,1)S(1)}, u32[]{:S(2)}, u32[]{:S(2)}) collective-permute-start(bf16[72,256]{1,0:T(8,128)(2,1)S(1)} %collective-permute-done.3), channel_id=1, source_target_pairs={{0,128},{32,160},{64,192},{96,224},{128,0},{160,32},{192,64},{224,... | collective-permute-start | bytes 110600 | tf_op jit(solution)/shard_map/ppermute | solution.py:15
  33.6 5.8 collective-permute-start.5
  39.4 0.6 copy-start.10
  40.1 167.4 %all-gather.5.cloned.1.call-start = ((), (), s32[]{:S(2)}) async-start(), calls=%async_computation | async-start | bytes 1216512 | tf_op jit(solution)/shard_map/all_gather | solution.py:75
  40.8 423.4 %all-gather.9.cloned.1.call-start = ((), (), s32[]{:S(2)}) async-start(), calls=%async_computation.3 | async-start | bytes 38928384 | tf_op jit(solution)/shard_map/all_gather | solution.py:102
  44.8 1.7 copy-start.3
  47.4 1.0 copy-start.13
  48.6 1.0 copy-start.11
  126.1 6.7 collective-permute-start.6
  142.6 7.4 copy-start.12
  142.6 9.9 %copy-start.14 = (bf16[1,16,16,2304]{3,2,1,0:T(8,128)(2,1)S(1)}, bf16[1,16,16,2304]{3,2,1,0:T(8,128)(2,1)}, u32[]{:S(2)}) copy-start(bf16[1,16,16,2304]{3,2,1,0:T(8,128)(2,1)} %constant_dynamic-update-slice_fusion.99) | copy-start | bytes 3538948
  145.7 7.4 copy-start.6
  145.7 6.9 collective-permute-start.7
  154.8 0.9 copy-start.1
  154.8 584.3 %all-reduce.14.cloned.1.call-start = ((), (), s32[]{:S(2)}) async-start(), calls=%async_computation.2 | async-start | bytes 2359296 | tf_op jit(solution)/shard_map/psum | solution.py:101
  156.0 1.7 copy-start.2
  161.9 1.9 copy-start.15
  210.3 7.5 %collective-permute-start = (bf16[1,16,16,256]{3,2,1,0:T(8,128)(2,1)S(1)}, bf16[1,16,16,256]{3,2,1,0:T(8,128)(2,1)S(1)}, u32[]{:S(2)}, u32[]{:S(2)}) collective-permute-start(bf16[1,16,16,256]{3,2,1,0:T(8,128)(2,1)S(1)} %bitcast.551), channel_id=1, source_target_pairs={{32,0},{64,32},{96,64},{128,96},{160,128},{192,160},{224,192},{256... | collective-permute-start | bytes 393224 | tf_op jit(solution)/shard_map/ppermute | solution.py:21
  231.2 7.1 collective-permute-start.1
  252.9 1.3 copy-start.16
  476.9 6.0 collective-permute-start.8
  482.9 7.1 collective-permute-start.9
  488.2 16.3 %copy-start.7 = (bf16[1,16,16,256]{3,2,1,0:T(8,128)(2,1)S(1)}, bf16[1,16,16,256]{3,2,1,0:T(8,128)(2,1)}, u32[]{:S(2)}) copy-start(bf16[1,16,16,256]{3,2,1,0:T(8,128)(2,1)} %copy-done.6) | copy-start | bytes 393220
  488.2 250.9 %copy-start.4 = (f32[1,72,256]{2,1,0:T(8,128)S(1)}, f32[1,72,256]{2,1,0:T(8,128)}, u32[]{:S(2)}) copy-start(f32[1,72,256]{2,1,0:T(8,128)} %param.11) | copy-start | bytes 221188
  488.3 250.9 %copy-start.8 = (f32[1,72,256]{2,1,0:T(8,128)S(1)}, f32[1,72,256]{2,1,0:T(8,128)}, u32[]{:S(2)}) copy-start(f32[1,72,256]{2,1,0:T(8,128)} %param.13) | copy-start | bytes 221188
  488.3 250.9 %copy-start.9 = (f32[1,72,256]{2,1,0:T(8,128)S(1)}, f32[1,72,256]{2,1,0:T(8,128)}, u32[]{:S(2)}) copy-start(f32[1,72,256]{2,1,0:T(8,128)} %param.12) | copy-start | bytes 221188
  489.9 10.6 %collective-permute-start.10 = (bf16[72,256]{1,0:T(8,128)(2,1)}, bf16[72,256]{1,0:T(8,128)(2,1)S(1)}, u32[]{:S(2)}, u32[]{:S(2)}) collective-permute-start(bf16[72,256]{1,0:T(8,128)(2,1)} %collective-permute-done.9), channel_id=1, source_target_pairs={{0,128},{32,160},{64,192},{96,224},{128,0},{160,32},{192,64},{224,... | collective-permute-start | bytes 110600 | tf_op jit(solution)/shard_map/ppermute | solution.py:15
  500.6 238.6 %collective-permute-start.11 = (bf16[72,256]{1,0:T(8,128)(2,1)S(1)}, bf16[72,256]{1,0:T(8,128)(2,1)S(1)}, u32[]{:S(2)}, u32[]{:S(2)}) collective-permute-start(bf16[72,256]{1,0:T(8,128)(2,1)S(1)} %collective-permute-done.10), channel_id=1, source_target_pairs={{0,256},{32,288},{64,320},{96,352},{128,384},{160,416},{192,448},{... | collective-permute-start | bytes 110600 | tf_op jit(solution)/shard_map/ppermute | solution.py:15
Sparse Core Ops, SparseCore 0:
  40.2 83.0 all-gather.6
  127.1 80.2 all-gather.4
  210.8 253.3 all-gather.8
  467.0 272.1 all-reduce.13
